TPU v7x, 32 devices: a whole 2x2x4 slice. The times are simulated.
32 devices in a mesh: row: 4 (over x, core), col: 8 (over z, y).
Axes of the slice: x: 2, y: 2, z: 4, core: 2. Of those that a mesh axis runs over, the one named last changes fastest.
Arguments:
- vectors: bfloat16 [1, 16, 4096], P(None, None, ('col', 'row')), may hold values from -110 to 110
- h_tiles: bfloat16 [1, 4, 256, 128, 128], P(None, 'row', 'col'), may hold values from -0.15625 to 0.15625
- h_list: int32 [1, 4, 256], P(None, 'row', 'col'), may hold values from -1 to 31, as said below
- j_tiles: bfloat16 [1, 4, 96, 128, 128], P(None, 'row', 'col'), may hold values from -0.25 to 0.25
- j_list: int32 [1, 4, 96], P(None, 'row', 'col'), may hold values from -1 to 63, as said below
Outputs:
- basis: float32 [1, 16, 4096], P(None, None, ('row', 'col'))
- transitions: float32 [1, 2, 16, 16], replicated
Inputs may be any that keep to these rules, and one draw needn't show every extreme that they name: `h_list`: each block's 32 entries list distinct tile positions first and then -1; at most 32 positions a block, and some block lists all 32. `j_list`: each block's 12 entries list distinct codes first and then -1; at most 12 codes a block, and some block lists all 12.
All inputs are finite; a program needn't handle non-finite values.
Results may differ from a plain program's by a relative error of at most 0.0003.
Values may be sent and summed in bfloat16 or wider, within the bound.
No kernel may reach another device: no remote copies, remote signals or barrier semaphores. Data moves between devices by JAX's collectives and lax.ppermute only.
A program may use at most 64 MiB of HBM per device.

v0:
```python
import math
import jax
import jax.numpy as jnp
from jax import lax
from jax.sharding import PartitionSpec as P

NSIT = 6
exact_precision = lax.Precision.HIGHEST


def local_product(tile_data, code_data, vector_block, operator_count, row_tiles):
    sector_count = tile_data.shape[0]
    tile_size = tile_data.shape[2]
    vector_count = vector_block.shape[1]
    column_tiles = vector_block.shape[2] // tile_size
    position_count = row_tiles * column_tiles
    column_vectors = vector_block.reshape(sector_count, vector_count, column_tiles, tile_size)
    places = code_data % position_count
    operator = code_data // position_count
    column_hot = (
        places[:, :, None] % column_tiles == jnp.arange(column_tiles)[None, None, :]
    ).astype(jnp.bfloat16)
    picked = jnp.einsum(
        "sqc,skcb->sqkb", column_hot, column_vectors, preferred_element_type=jnp.float32
    ).astype(jnp.bfloat16)
    product = jnp.einsum("sqab,sqkb->sqka", tile_data, picked, preferred_element_type=jnp.float32)
    row_hot = (
        (operator[:, :, None, None] == jnp.arange(operator_count)[None, None, :, None])
        & (places[:, :, None, None] // column_tiles == jnp.arange(row_tiles)[None, None, None, :])
        & (code_data[:, :, None, None] >= 0)
    ).astype(jnp.float32)
    result = jnp.einsum("sqor,sqka->sokra", row_hot, product, precision=exact_precision)
    return result.reshape(sector_count, operator_count * vector_count, row_tiles * tile_size)


def inverse_root_of(gram, vector_count):
    scale = jnp.sqrt(jnp.sum(gram * gram, axis=(1, 2), keepdims=True) + 1e-06)
    iterate = gram / scale
    identity = jnp.eye(vector_count, dtype=jnp.float32)[None]
    inverse_root = identity
    for iteration in range(NSIT):
        middle = 1.5 * identity - 0.5 * jnp.einsum(
            "skm,sml->skl", inverse_root, iterate, precision=exact_precision
        )
        iterate = jnp.einsum("skm,sml->skl", iterate, middle, precision=exact_precision)
        inverse_root = jnp.einsum("skm,sml->skl", middle, inverse_root, precision=exact_precision)
    return (inverse_root, scale)


def per_device(vectors, h_tiles, h_list, j_tiles, j_list):
    sector_count = vectors.shape[0]
    vector_count = vectors.shape[1]
    tile_size = h_tiles.shape[-1]
    block_rows = vectors.shape[2] * lax.axis_size("col")
    total_rows = block_rows * lax.axis_size("row")
    row_tiles = block_rows // tile_size
    vector_block = lax.all_gather(vectors, "row", axis=2, tiled=True)
    h_part = local_product(
        h_tiles.reshape(sector_count, -1, tile_size, tile_size),
        h_list.reshape(sector_count, -1),
        vector_block,
        1,
        row_tiles,
    )
    j_part = local_product(
        j_tiles.reshape(sector_count, -1, tile_size, tile_size),
        j_list.reshape(sector_count, -1),
        vector_block,
        2,
        row_tiles,
    )
    projected, applied = (
        lax.psum_scatter(h_part, "col", scatter_dimension=2, tiled=True),
        lax.psum_scatter(j_part, "col", scatter_dimension=2, tiled=True),
    )
    gram_part = jnp.einsum("skp,slp->skl", projected, projected, precision=exact_precision)
    gram = lax.psum(gram_part, ("row", "col"))
    inverse_root, scale = inverse_root_of(gram, vector_count)
    basis = jnp.sqrt(total_rows / scale) * jnp.einsum(
        "smk,smp->skp", inverse_root, projected, precision=exact_precision
    )
    element_part = jnp.einsum("skp,smp->skm", basis, applied, precision=exact_precision)
    elements = lax.psum(element_part, ("row", "col")) / math.sqrt(total_rows)
    elements = elements.reshape(sector_count, vector_count, 2, vector_count).transpose(0, 2, 1, 3)
    return (basis, elements)


def solution(mesh):
    return jax.shard_map(
        per_device,
        mesh=mesh,
        in_specs=(
            P(None, None, ("col", "row")),
            P(None, "row", "col", None, None),
            P(None, "row", "col"),
            P(None, "row", "col", None, None),
            P(None, "row", "col"),
        ),
        out_specs=(P(None, None, ("row", "col")), P()),
        check_vma=False,
    )
```

profile of v0, /device:TPU:0, one launch (start us, length us, event | category | flops | bytes accessed | tf_op | source)
XLA Modules:
  0.0 189.2 jit_solution(17668249501114527060)
XLA Ops:
  7.2 0.7 fusion.38
  8.0 6.4 %all_gather.3 = bf16[1,16,512]{2,1,0:T(8,128)(2,1)S(1)} all-gather(bf16[1,16,128]{2,1,0:T(8,128)(2,1)} %param.5), channel_id=1, replica_groups=mesh['row'=4,'col'=8] {'row'}, dimensions={2}, use_global_device_ids=true | all-gather | bytes 20480 | tf_op jit(solution)/shard_map/all_gather | solution.py:57
  14.4 0.2 convolution_convert_fusion
  14.7 0.6 fusion.6
  15.3 0.3 convolution_bitcast_fusion.2
  15.6 0.6 reshape.796
  16.3 0.7 bitcast_compare_fusion
  17.0 0.7 and_select_fusion.1
  17.7 0.2 convolution_convert_fusion.1
  17.9 1.3 convolution_bitcast_fusion.1
  19.2 0.3 convolution_bitcast_fusion
  19.5 13.7 %copy.19 = f32[1,32,1024]{0,1,2:T(8,128)} copy(f32[1,32,1024]{2,0,1:T(1,128)S(1)} %bitcast.122) | data formatting | bytes 262144
  33.2 9.0 %bitcast_reduce_fusion = f32[1024,32]{1,0:T(8,128)} fusion(f32[1,32,1024]{0,1,2:T(8,128)} %copy.19), kind=kLoop, calls=%fused_computation | loop fusion | bytes 262144
  42.2 30.7 %reduce-scatter.5.cloned.1.call-done = f32[1,16,128]{2,1,0:T(8,128)} async-done(((f32[1,16,1024]{2,1,0:T(8,128)}), f32[1,16,128]{2,1,0:T(8,128)}) %reduce-scatter.5.cloned.1.call-update) | async-done | bytes 8208 | tf_op jit(solution)/shard_map/reduce_scatter | solution.py:73
  72.9 0.9 convolution_bitcast_fusion.4
  73.8 40.3 %psum.14 = f32[1,16,16]{2,1,0:T(8,128)S(1)} all-reduce(f32[1,16,16]{2,1,0:T(8,128)S(1)} %convolution_bitcast_fusion.4), channel_id=1, replica_groups=mesh['row'=4,'col'=8] {'row','col'}, use_global_device_ids=true, to_apply=%region_1.2 | all-reduce | flops 256 | bytes 2048 | tf_op jit(solution)/shard_map/psum | solution.py:77
  114.2 0.6 multiply_reduce_fusion
  115.6 0.1 fusion.13
  117.9 0.9 convolution_multiply_fusion
  118.8 19.9 %reduce-scatter.7.cloned.1.call-done = f32[128,32]{1,0:T(8,128)} async-done(((f32[1024,32]{1,0:T(8,128)}), f32[128,32]{1,0:T(8,128)}) %reduce-scatter.7.cloned.1.call-update) | async-done | bytes 16400
  138.7 1.4 reshape_bitcast_fusion
  140.2 1.3 copy.20
  141.6 40.0 %psum.15 = f32[1,16,32]{2,1,0:T(8,128)S(1)} all-reduce(f32[1,16,32]{2,1,0:T(8,128)S(1)} %convolution_bitcast_fusion.3), channel_id=1, replica_groups=mesh['row'=4,'col'=8] {'row','col'}, use_global_device_ids=true, to_apply=%region_4.5 | all-reduce | flops 512 | bytes 4096 | tf_op jit(solution)/shard_map/psum | solution.py:83
  181.7 0.6 copy.30
  (35 shorter events, 2.6 us)
Async XLA Ops:
  7.2 7.5 %copy-start = (bf16[1,1,32,128,128]{4,3,2,1,0:T(8,128)(2,1)S(1)}, bf16[1,1,32,128,128]{4,3,2,1,0:T(8,128)(2,1)}, u32[]{:S(2)}) copy-start(bf16[1,1,32,128,128]{4,3,2,1,0:T(8,128)(2,1)} %param.6) | copy-start | bytes 3145732
  7.2 65.8 %reduce-scatter.5.cloned.1.call-start = ((), (), s32[]{:S(2)}) async-start(), calls=%async_computation.2 | async-start | bytes 73728 | tf_op jit(solution)/shard_map/reduce_scatter | solution.py:73
  16.3 122.5 %reduce-scatter.7.cloned.1.call-start = ((), (), s32[]{:S(2)}) async-start(), calls=%async_computation.3 | async-start | bytes 589824
  118.8 63.5 %copy-start.1 = (f32[16,128]{1,0:T(8,128)}, f32[16,128]{1,0:T(8,128)S(1)}, u32[]{:S(2)}) copy-start(f32[16,128]{1,0:T(8,128)S(1)} %convolution_multiply_fusion) | copy-start | bytes 24580
Sparse Core Ops, SparseCore 0:
  16.4 56.5 reduce-scatter.4
  76.3 62.3 reduce-scatter.6
where the time goes:
time: 190 us; the launch traced here: 189 us
  blocking collectives  86.8 us (46%)
  waiting for transfers between devices  50.7 us (27%)
  local copies, waits for them, and re-layouts  26.9 us (14%)
  between operations  14.9 us (8%)
  matrix products  7.18 us (4%)
  other arithmetic  2.72 us (1%)
    psum x1, blocking collectives, per_device(): gram = lax.psum(gram_part, ('row', 'col'))  40.3 us
    psum x1, blocking collectives, per_device(): elements = lax.psum(element_part, ('row', 'col')) / math.sqrt(total_rows)  40 us
    reduce_scatter x1, waiting for transfers between devices, per_device(): lax.psum_scatter(h_part, 'col', scatter_dimension=2, tiled=True)  30.7 us
    unnamed x8, local copies, waits for them, and re-layouts  25.5 us
    unnamed x3, waiting for transfers between devices  20 us
    all_gather x1, blocking collectives, per_device(): vector_block = lax.all_gather(vectors, 'row', axis=2, tiled=True)  6.39 us
  transfers between devices with their start and end apart: 2, of which 2 were waited for; matrix products, arithmetic and copies ran while one was open for 16% of the time, Pallas kernels for 0%

commit v1 on v0

--- a/solution.py
+++ b/solution.py
@@ -6,6 +6,12 @@
 
 NSIT = 6
 exact_precision = lax.Precision.HIGHEST
+
+
+def summed_here(value, mesh_axis):
+    pieces = lax.all_gather(value, mesh_axis, axis=0, tiled=False)
+    total = pieces.sum(axis=0)
+    return total
 
 
 def local_product(tile_data, code_data, vector_block, operator_count, row_tiles):
@@ -80,7 +86,7 @@
         "smk,smp->skp", inverse_root, projected, precision=exact_precision
     )
     element_part = jnp.einsum("skp,smp->skm", basis, applied, precision=exact_precision)
-    elements = lax.psum(element_part, ("row", "col")) / math.sqrt(total_rows)
+    elements = summed_here(element_part, ("row", "col")) / math.sqrt(total_rows)
     elements = elements.reshape(sector_count, vector_count, 2, vector_count).transpose(0, 2, 1, 3)
     return (basis, elements)
 

time: 190 us -> 216 us (1.14)
  blocking collectives: 86.8 us -> 113 us
    all_gather x0 -> x1, blocking collectives: none -> 66 us  [summed_here(): pieces = lax.all_gather(value, mesh_axis, axis=0, tiled=False)]
    psum x1 -> x0, blocking collectives: 40 us -> none  [per_device(): elements = lax.psum(element_part, ('row', 'col')) / math.sqrt(total_rows)]
    unnamed x8 -> x9, local copies, waits for them, and re-layouts: 25.5 us -> 26.1 us
  transfers between devices with their start and end apart: 2 -> 2, of which waited for: 2 -> 2; matrix products, arithmetic and copies ran while one was open for 16% -> 14% of each run, Pallas kernels for 0% -> 0%
where the time goes in v1:
time: 216 us; the launch traced here: 215 us
  blocking collectives  113 us (52%)
  waiting for transfers between devices  50.7 us (23%)
  local copies, waits for them, and re-layouts  26.9 us (12%)
  between operations  14.9 us (7%)
  matrix products  7.18 us (3%)
  other arithmetic  2.76 us (1%)
    all_gather x1, blocking collectives, summed_here(): pieces = lax.all_gather(value, mesh_axis, axis=0, tiled=False)  66 us
    psum x1, blocking collectives, per_device(): gram = lax.psum(gram_part, ('row', 'col'))  40.3 us
    reduce_scatter x1, waiting for transfers between devices, per_device(): lax.psum_scatter(h_part, 'col', scatter_dimension=2, tiled=True)  30.7 us
    unnamed x9, local copies, waits for them, and re-layouts  26.1 us
    unnamed x3, waiting for transfers between devices  20 us
    all_gather x1, blocking collectives, per_device(): vector_block = lax.all_gather(vectors, 'row', axis=2, tiled=True)  6.39 us
  transfers between devices with their start and end apart: 2, of which 2 were waited for; matrix products, arithmetic and copies ran while one was open for 14% of the time, Pallas kernels for 0%

profile of v1, /device:TPU:0, one launch (start us, length us, event | category | flops | bytes accessed | tf_op | source)
XLA Modules:
  0.0 215.2 jit_solution(10224163436881815991)
XLA Ops:
  7.2 0.7 fusion.38
  8.0 6.4 %all_gather.9 = bf16[1,16,512]{2,1,0:T(8,128)(2,1)S(1)} all-gather(bf16[1,16,128]{2,1,0:T(8,128)(2,1)} %param.5), channel_id=1, replica_groups=mesh['row'=4,'col'=8] {'row'}, dimensions={2}, use_global_device_ids=true | all-gather | bytes 20480 | tf_op jit(solution)/shard_map/all_gather | solution.py:63
  14.4 0.2 convolution_convert_fusion
  14.7 0.6 fusion.6
  15.3 0.3 convolution_bitcast_fusion.2
  15.6 0.6 reshape.811
  16.3 0.7 bitcast_compare_fusion
  17.0 0.7 and_select_fusion.1
  17.7 0.2 convolution_convert_fusion.1
  17.9 1.3 convolution_bitcast_fusion.1
  19.2 0.3 convolution_bitcast_fusion
  19.5 13.7 %copy.18 = f32[1,32,1024]{0,1,2:T(8,128)} copy(f32[1,32,1024]{2,0,1:T(1,128)S(1)} %bitcast.120) | data formatting | bytes 262144
  33.2 9.0 %bitcast_reduce_fusion = f32[1024,32]{1,0:T(8,128)} fusion(f32[1,32,1024]{0,1,2:T(8,128)} %copy.18), kind=kLoop, calls=%fused_computation | loop fusion | bytes 262144
  42.2 30.7 %reduce-scatter.5.cloned.1.call-done = f32[1,16,128]{2,1,0:T(8,128)} async-done(((f32[1,16,1024]{2,1,0:T(8,128)}), f32[1,16,128]{2,1,0:T(8,128)}) %reduce-scatter.5.cloned.1.call-update) | async-done | bytes 8208 | tf_op jit(solution)/shard_map/reduce_scatter | solution.py:79
  72.9 0.9 convolution_bitcast_fusion.3
  73.8 40.3 %psum.7 = f32[1,16,16]{2,1,0:T(8,128)S(1)} all-reduce(f32[1,16,16]{2,1,0:T(8,128)S(1)} %convolution_bitcast_fusion.3), channel_id=1, replica_groups=mesh['row'=4,'col'=8] {'row','col'}, use_global_device_ids=true, to_apply=%region_1.2 | all-reduce | flops 256 | bytes 2048 | tf_op jit(solution)/shard_map/psum | solution.py:83
  114.2 0.6 multiply_reduce_fusion
  115.6 0.1 fusion.13
  117.9 0.9 convolution_multiply_fusion
  118.8 19.9 %reduce-scatter.7.cloned.1.call-done = f32[128,32]{1,0:T(8,128)} async-done(((f32[1024,32]{1,0:T(8,128)}), f32[128,32]{1,0:T(8,128)}) %reduce-scatter.7.cloned.1.call-update) | async-done | bytes 16400
  138.7 1.4 reshape_bitcast_fusion
  140.2 1.3 copy.19
  141.6 66.0 %all-gather = f32[512,32]{1,0:T(8,128)S(1)} all-gather(f32[16,32]{1,0:T(8,128)S(1)} %fusion.48), channel_id=2, replica_groups=mesh['row'=4,'col'=8] {'row','col'}, dimensions={0}, use_global_device_ids=true | all-gather | bytes 67584 | tf_op jit(solution)/shard_map/all_gather | solution.py:12
  207.7 0.6 copy.14
  (36 shorter events, 2.6 us)
Async XLA Ops:
  7.2 7.5 %copy-start = (bf16[1,1,32,128,128]{4,3,2,1,0:T(8,128)(2,1)S(1)}, bf16[1,1,32,128,128]{4,3,2,1,0:T(8,128)(2,1)}, u32[]{:S(2)}) copy-start(bf16[1,1,32,128,128]{4,3,2,1,0:T(8,128)(2,1)} %param.6) | copy-start | bytes 3145732
  7.2 65.8 %reduce-scatter.5.cloned.1.call-start = ((), (), s32[]{:S(2)}) async-start(), calls=%async_computation.2 | async-start | bytes 73728 | tf_op jit(solution)/shard_map/reduce_scatter | solution.py:79
  16.3 122.5 %reduce-scatter.7.cloned.1.call-start = ((), (), s32[]{:S(2)}) async-start(), calls=%async_computation.3 | async-start | bytes 589824
  118.8 89.5 %copy-start.1 = (f32[16,128]{1,0:T(8,128)}, f32[16,128]{1,0:T(8,128)S(1)}, u32[]{:S(2)}) copy-start(f32[16,128]{1,0:T(8,128)S(1)} %convolution_multiply_fusion) | copy-start | bytes 24580
Sparse Core Ops, SparseCore 0:
  16.4 56.5 reduce-scatter.4
  76.3 62.3 reduce-scatter.6
